TPU v7x, 256 devices: a whole 4x4x8 slice. The times are simulated.
256 devices in a mesh: row: 8 (over x, core), col: 32 (over z, y).
Axes of the slice: x: 4, y: 4, z: 8, core: 2. Of those that a mesh axis runs over, the one named last changes fastest.
Arguments:
- panel: bfloat16 [65536, 512], P('row', 'col'), may hold values from -0.0234375 to 0.0234375
- pheno: bfloat16 [65536, 8192], P('row', 'col'), may hold values from -48 to 48
- kin_values: float32 [512], replicated, may hold values from 0.1 to 10
- trait_values: float32 [128], replicated, may hold values from 0.1 to 10
- trait_basis: float32 [128, 128], replicated, may hold values from -0.5 to 0.5
Outputs:
- coeffs: float32 [512, 8192], P('row', 'col')
- genetic: bfloat16 [65536, 8192], P('row', 'col')
All inputs are finite; a program needn't handle non-finite values.
Results may differ from a plain program's by a relative error of at most 0.0049.
Values may be sent and summed in bfloat16 or wider, within the bound.
No kernel may reach another device: no remote copies, remote signals or barrier semaphores. Data moves between devices by JAX's collectives and lax.ppermute only.
A program may use at most 64 MiB of HBM per device.

v0:
```python
import jax
import jax.numpy as jnp
from jax import lax
from jax.sharding import PartitionSpec as P

TRAITS = 128
SETS_DEV = 2


def cut_along(shard, dim, count):
    before, after = (shard.shape[:dim], shard.shape[dim + 1 :])
    return jnp.moveaxis(shard.reshape(*before, count, -1, *after), dim, 0)


def sum_at_owner(shard, axis, dim):
    count = lax.axis_size(axis)
    pieces = lax.all_to_all(cut_along(shard, dim, count), axis, 0, 0, tiled=True)
    return jnp.sum(pieces, axis=0)


def laid_out(pieces, dim):
    dims = list(pieces.shape[1:])
    dims[dim] *= pieces.shape[0]
    return jnp.moveaxis(pieces, 0, dim).reshape(dims)


def copy_for_each(shard, axis):
    count = lax.axis_size(axis)
    return lax.all_to_all(
        jnp.broadcast_to(shard[None], (count, *shard.shape)), axis, 0, 0, tiled=True
    )


def gather_directly(shard, axis, dim):
    return laid_out(copy_for_each(shard, axis), dim)


def local(panel, pheno, kin_values, trait_values, trait_basis):
    col_count = lax.axis_size("col")
    columns = pheno.shape[1]
    traits_here = TRAITS // col_count
    set_count = SETS_DEV * col_count
    whole_panel = lax.all_gather(panel, "col", axis=1, tiled=True)
    partial_value = lax.dot_general(
        whole_panel, pheno, (((0,), (0,)), ((), ())), preferred_element_type=jnp.float32
    )
    summed = sum_at_owner(partial_value, "row", 0)
    first_row = lax.axis_index("row") * summed.shape[0]
    share_rows = summed.shape[0]
    by_trait = summed.reshape(share_rows, traits_here, set_count).transpose(0, 2, 1)
    by_trait = by_trait.reshape(share_rows, set_count * traits_here)
    grouped = lax.all_to_all(by_trait, "col", split_axis=1, concat_axis=1, tiled=True)
    grouped = grouped.reshape(share_rows, col_count, SETS_DEV, traits_here).transpose(0, 2, 1, 3)
    grouped = grouped.reshape(share_rows, SETS_DEV, TRAITS)
    rotated = jnp.einsum("rst,tj->rsj", grouped, trait_basis, precision=lax.Precision.HIGHEST)
    kin_rows = lax.dynamic_slice_in_dim(kin_values, first_row, share_rows, 0)
    product = kin_rows[:, None] * trait_values[None, :]
    scaled = rotated * (product / (product + 1.0))[:, None, :]
    unrotated = jnp.einsum("rsj,tj->rst", scaled, trait_basis, precision=lax.Precision.HIGHEST)
    outgoing = unrotated.reshape(share_rows, SETS_DEV, col_count, traits_here).transpose(0, 2, 1, 3)
    outgoing = outgoing.reshape(share_rows, col_count * SETS_DEV * traits_here)
    returned = lax.all_to_all(outgoing, "col", split_axis=1, concat_axis=1, tiled=True)
    coeffs = returned.reshape(share_rows, set_count, traits_here).transpose(0, 2, 1)
    coeffs = coeffs.reshape(share_rows, columns)
    coeffs_low = gather_directly(coeffs.astype(jnp.bfloat16), "row", 0)
    genetic = jnp.dot(whole_panel, coeffs_low, preferred_element_type=jnp.float32)
    return (coeffs, genetic.astype(jnp.bfloat16))


def solution(mesh):
    return jax.shard_map(
        local,
        mesh=mesh,
        in_specs=(P("row", "col"), P("row", "col"), P(), P(), P()),
        out_specs=(P("row", "col"), P("row", "col")),
        check_vma=False,
    )
```

profile of v0, /device:TPU:1, one launch (start us, length us, event | category | flops | bytes accessed | tf_op | source)
XLA Modules:
  0.0 199.2 jit_solution(6438156583780600088)
XLA Ops:
  7.2 0.0 copy-start
  7.2 0.0 all-gather.2.cloned.1.call-start
  7.2 0.7 all-gather.2.cloned.1.call-update
  7.9 0.0 copy-start.2
  7.9 104.7 %all-gather.2.cloned.1.call-done = bf16[8192,512]{0,1:T(8,128)(2,1)} async-done(((bf16[8192,16]{0,1:T(8,128)(2,1)}), bf16[8192,512]{0,1:T(8,128)(2,1)}) %all-gather.2.cloned.1.call-update) | async-done | bytes 8388624 | tf_op jit(solution)/shard_map/all_gather | solution.py:43
  112.6 7.7 %fusion.4 = f32[512,256]{1,0:T(8,128)} fusion(bf16[8192,512]{0,1:T(8,128)(2,1)} %all-gather.2.cloned.1.call-done, bf16[8192,256]{1,0:T(8,128)(2,1)} %param.6), kind=kOutput, calls=%fused_computation.9 | convolution fusion | flops 2147483648 | bytes 13107200 | tf_op jit(solution)/shard_map/dot_general | solution.py:44
  120.3 5.3 %all-to-all-start = ((f32[8,64,256]{2,1,0:T(8,128)}), f32[8,64,256]{2,1,0:T(8,128)S(1)}, u32[]{:S(2)}, u32[]{:S(2)}) async-start(f32[8,64,256]{2,1,0:T(8,128)} %bitcast), calls=%async_computation | async-start | bytes 1048576 | tf_op jit(solution)/shard_map/all_to_all | solution.py:17
  125.6 0.8 dynamic_slice.3
  126.4 8.7 %all-to-all-done = f32[8,64,256]{2,1,0:T(8,128)S(1)} async-done(((f32[8,64,256]{2,1,0:T(8,128)}), f32[8,64,256]{2,1,0:T(8,128)S(1)}, u32[]{:S(2)}, u32[]{:S(2)}) %all-to-all-start) | async-done | bytes 524320 | tf_op jit(solution)/shard_map/all_to_all | solution.py:17
  135.1 0.1 reshape.69
  135.2 0.1 copy.23
  135.4 0.8 reshape.77
  136.1 5.3 %all-to-all-start.1 = ((f32[32,1,512]{2,1,0:T(1,128)}), f32[32,1,512]{2,1,0:T(1,128)S(1)}, u32[]{:S(2)}, u32[]{:S(2)}) async-start(f32[32,1,512]{2,1,0:T(1,128)} %reshape.77), calls=%async_computation.1 | async-start | bytes 131072 | tf_op jit(solution)/shard_map/all_to_all | solution.py:52
  141.5 0.0 copy-done.2
  141.5 0.1 add_divide_fusion
  141.6 8.7 %all-to-all-done.1 = f32[32,1,512]{2,1,0:T(1,128)S(1)} async-done(((f32[32,1,512]{2,1,0:T(1,128)}), f32[32,1,512]{2,1,0:T(1,128)S(1)}, u32[]{:S(2)}, u32[]{:S(2)}) %all-to-all-start.1) | async-done | bytes 65568 | tf_op jit(solution)/shard_map/all_to_all | solution.py:52
  150.3 0.5 broadcast.18
  150.8 0.8 reduce
  151.7 0.1 reshape.78
  151.8 0.1 copy.25
  151.9 0.0 copy-done
  151.9 0.4 convolution_multiply_fusion
  152.3 0.3 fusion.1
  152.6 0.1 copy.35
  152.7 0.1 reshape.79
  152.8 12.0 %all_to_all.28 = f32[32,1,512]{2,1,0:T(1,128)S(1)} all-to-all(f32[32,1,512]{2,1,0:T(1,128)S(1)} %reshape.79), channel_id=1, replica_groups=mesh['row'=8,'col'=32] {'col'}, dimensions={0} | all-to-all | bytes 131072 | tf_op jit(solution)/shard_map/all_to_all | solution.py:62
  164.8 0.8 reduce.1
  165.6 0.1 reshape.80
  165.7 0.1 copy.30
  165.8 0.1 reshape.74
  166.0 0.0 copy-start.1
  166.0 12.3 %all_to_all.29 = bf16[8,64,256]{2,1,0:T(8,128)(2,1)S(1)} all-to-all(bf16[8,64,256]{2,1,0:T(8,128)(2,1)S(1)} %broadcast_in_dim.2), channel_id=1, replica_groups=mesh['row'=8,'col'=32] {'row'}, dimensions={0} | all-to-all | bytes 524288 | tf_op jit(solution)/shard_map/all_to_all | solution.py:29
  178.3 7.7 %fusion = bf16[8192,256]{0,1:T(8,128)(2,1)} fusion(bf16[512,256]{1,0:T(8,128)(2,1)S(1)} %bitcast.37, bf16[8192,512]{0,1:T(8,128)(2,1)} %all-gather.2.cloned.1.call-done), kind=kOutput, calls=%fused_computation.1 | convolution fusion | flops 2149580800 | bytes 12845056 | tf_op jit(solution)/shard_map/dot_general | solution.py:66
  186.0 6.4 %copy.31 = bf16[8192,256]{1,0:T(8,128)(2,1)} copy(bf16[8192,256]{0,1:T(8,128)(2,1)} %fusion) | data formatting | bytes 8388608
  192.4 0.0 copy-done.1
  (6 shorter events, 0.1 us)
Async XLA Ops:
  7.2 144.7 %copy-start = (f32[128,128]{1,0:T(8,128)S(1)}, f32[128,128]{1,0:T(8,128)}, u32[]{:S(2)}) copy-start(f32[128,128]{1,0:T(8,128)} %param.9) | copy-start | bytes 196612
  7.2 105.4 %all-gather.2.cloned.1.call-start = ((), (), s32[]{:S(2)}) async-start(), calls=%async_computation.4 | async-start | bytes 8650752 | tf_op jit(solution)/shard_map/all_gather | solution.py:43
  7.9 133.6 %copy-start.2 = (f32[128]{0:T(128)S(1)}, f32[128]{0:T(128)}, u32[]{:S(2)}) copy-start(f32[128]{0:T(128)} %param.8) | copy-start | bytes 1540
  120.3 14.8 %all-to-all-start = ((f32[8,64,256]{2,1,0:T(8,128)}), f32[8,64,256]{2,1,0:T(8,128)S(1)}, u32[]{:S(2)}, u32[]{:S(2)}) async-start(f32[8,64,256]{2,1,0:T(8,128)} %bitcast), calls=%async_computation | async-start | bytes 1048576 | tf_op jit(solution)/shard_map/all_to_all | solution.py:17
  136.1 14.2 %all-to-all-start.1 = ((f32[32,1,512]{2,1,0:T(1,128)}), f32[32,1,512]{2,1,0:T(1,128)S(1)}, u32[]{:S(2)}, u32[]{:S(2)}) async-start(f32[32,1,512]{2,1,0:T(1,128)} %reshape.77), calls=%async_computation.1 | async-start | bytes 131072 | tf_op jit(solution)/shard_map/all_to_all | solution.py:52
  166.0 26.4 %copy-start.1 = (f32[64,256]{1,0:T(8,128)}, f32[64,256]{1,0:T(8,128)S(1)}, u32[]{:S(2)}) copy-start(f32[64,256]{1,0:T(8,128)S(1)} %reshape.74) | copy-start | bytes 196612
Sparse Core Ops, SparseCore 0:
  10.6 101.9 all-gather.1
where the time goes:
time: 200 us; the launch traced here: 199 us
  waiting for transfers between devices  123 us (62%)
  blocking collectives  24.2 us (12%)
  matrix products  16.1 us (8%)
  between operations  14.2 us (7%)
  starting transfers between devices  10.7 us (5%)
  local copies, waits for them, and re-layouts  9.41 us (5%)
    all_gather x1, waiting for transfers between devices, local(): whole_panel = lax.all_gather(panel, 'col', axis=1, tiled=True)  105 us
    all_to_all x1, blocking collectives, copy_for_each(): lax.all_to_all(jnp.broadcast_to(shard[None], (count, *shard.shape)), axis...  12.3 us
    all_to_all x1, blocking collectives, local(): lax.all_to_all(outgoing, 'col', split_axis=1, concat_axis=1, tiled=True)  12 us
    all_to_all x1, waiting for transfers between devices, local(): lax.all_to_all(by_trait, 'col', split_axis=1, concat_axis=1, tiled=True)  8.74 us
    all_to_all x1, waiting for transfers between devices, sum_at_owner(): lax.all_to_all(cut_along(shard, dim, count), axis, 0, 0, tiled=True)  8.73 us
    dot_general x1, matrix products, local(): jnp.dot(whole_panel, coeffs_low, preferred_element_type=jnp.float32)  7.71 us
    dot_general x1, matrix products, local(): lax.dot_general(whole_panel, pheno, (((0,), (0,)), ((), ())), preferred_e...  7.7 us
    unnamed x12, local copies, waits for them, and re-layouts  7.44 us
  transfers between devices with their start and end apart: 3, of which 3 were waited for; matrix products, arithmetic and copies ran while one was open for 0% of the time, Pallas kernels for 0%

commit v1 on v0

--- a/solution.py
+++ b/solution.py
@@ -40,7 +40,9 @@
     columns = pheno.shape[1]
     traits_here = TRAITS // col_count
     set_count = SETS_DEV * col_count
-    whole_panel = lax.all_gather(panel, "col", axis=1, tiled=True)
+    whole_panel = jnp.concatenate(
+        lax.all_to_all(jnp.stack([panel] * lax.axis_size("col")), "col", 0, 0), axis=1
+    )
     partial_value = lax.dot_general(
         whole_panel, pheno, (((0,), (0,)), ((), ())), preferred_element_type=jnp.float32
     )

time: 200 us -> 279 us (1.40)
  blocking collectives: 24.2 us -> 220 us
  waiting for transfers between devices: 123 us -> 17.5 us
  between operations: 14.2 us -> 0.8 us
  local copies, waits for them, and re-layouts: 9.41 us -> 14.6 us
  matrix products: 16.1 us -> 11.6 us
    all_to_all x0 -> x1, blocking collectives: none -> 196 us  [local(): lax.all_to_all(jnp.stack([panel] * lax.axis_size('col')), 'col', 0, 0)]
    all_gather x1 -> x0, waiting for transfers between devices: 105 us -> none  [local(): whole_panel = lax.all_gather(panel, 'col', axis=1, tiled=True)]
    dot_general x1, matrix products: 7.7 us -> 3.12 us  [local(): lax.dot_general(whole_panel, pheno, (((0,), (0,)), ((), ())), preferred_e...]
    unnamed x12 -> x16, local copies, waits for them, and re-layouts: 7.44 us -> 10.7 us
  transfers between devices with their start and end apart: 3 -> 2, of which waited for: 3 -> 2; matrix products, arithmetic and copies ran while one was open for 0% -> 0% of each run, Pallas kernels for 0% -> 0%
where the time goes in v1:
time: 279 us; the launch traced here: 278 us
  blocking collectives  220 us (79%)
  waiting for transfers between devices  17.5 us (6%)
  local copies, waits for them, and re-layouts  14.6 us (5%)
  starting transfers between devices  12.4 us (4%)
  matrix products  11.6 us (4%)
    all_to_all x1, blocking collectives, local(): lax.all_to_all(jnp.stack([panel] * lax.axis_size('col')), 'col', 0, 0)  196 us
    all_to_all x1, blocking collectives, copy_for_each(): lax.all_to_all(jnp.broadcast_to(shard[None], (count, *shard.shape)), axis...  12.3 us
    all_to_all x1, blocking collectives, local(): lax.all_to_all(outgoing, 'col', split_axis=1, concat_axis=1, tiled=True)  12 us
    unnamed x16, local copies, waits for them, and re-layouts  10.7 us
    all_to_all x1, waiting for transfers between devices, local(): lax.all_to_all(by_trait, 'col', split_axis=1, concat_axis=1, tiled=True)  8.74 us
    all_to_all x1, waiting for transfers between devices, sum_at_owner(): lax.all_to_all(cut_along(shard, dim, count), axis, 0, 0, tiled=True)  8.73 us
    dot_general x1, matrix products, local(): jnp.dot(whole_panel, coeffs_low, preferred_element_type=jnp.float32)  7.73 us
    all_to_all x1, starting transfers between devices, sum_at_owner(): lax.all_to_all(cut_along(shard, dim, count), axis, 0, 0, tiled=True)  7.13 us
  transfers between devices with their start and end apart: 2, of which 2 were waited for; matrix products, arithmetic and copies ran while one was open for 0% of the time, Pallas kernels for 0%

profile of v1, /device:TPU:1, one launch (start us, length us, event | category | flops | bytes accessed | tf_op | source)
XLA Modules:
  0.0 278.4 jit_solution(1168422730093412155)
XLA Ops:
  0.6 0.0 copy-start
  0.6 2.0 stack.2
  2.6 0.0 copy-start.4
  2.6 195.6 %all_to_all.33 = bf16[32,8192,16]{1,2,0:T(8,128)(2,1)S(1)} all-to-all(bf16[32,8192,16]{1,2,0:T(8,128)(2,1)S(1)} %stack.2), channel_id=1, replica_groups=mesh['row'=8,'col'=32] {'col'}, dimensions={0} | all-to-all | bytes 16777216 | tf_op jit(solution)/shard_map/all_to_all | solution.py:44
  198.2 0.0 copy-start.1
  198.3 3.2 %copy-done.1 = bf16[32,8192,16]{1,2,0:T(8,128)(2,1)} copy-done((bf16[32,8192,16]{1,2,0:T(8,128)(2,1)}, bf16[32,8192,16]{1,2,0:T(8,128)(2,1)S(1)}, u32[]{:S(2)}) %copy-start.1) | copy-done | bytes 8388632
  201.5 0.0 copy-done.4
  201.5 0.0 copy-start.3
  201.5 3.1 %fusion.1 = f32[8,64,256]{2,1,0:T(8,128)} fusion(bf16[8,64,8192]{2,1,0:T(8,128)(2,1)S(1)} %bitcast.45, bf16[8192,256]{1,0:T(8,128)(2,1)S(1)} %copy-done.4), kind=kOutput, calls=%fused_computation.2 | convolution fusion | flops 2147483648 | bytes 13107200 | tf_op jit(solution)/shard_map/dot_general | solution.py:46
  204.6 7.1 %all-to-all-start.1 = ((f32[8,64,256]{2,1,0:T(8,128)}), f32[8,64,256]{2,1,0:T(8,128)S(1)}, u32[]{:S(2)}, u32[]{:S(2)}) async-start(f32[8,64,256]{2,1,0:T(8,128)} %fusion.1), calls=%async_computation.1 | async-start | bytes 1048576 | tf_op jit(solution)/shard_map/all_to_all | solution.py:17
  211.7 0.8 dynamic_slice.3
  212.5 8.7 %all-to-all-done.1 = f32[8,64,256]{2,1,0:T(8,128)S(1)} async-done(((f32[8,64,256]{2,1,0:T(8,128)}), f32[8,64,256]{2,1,0:T(8,128)S(1)}, u32[]{:S(2)}, u32[]{:S(2)}) %all-to-all-start.1) | async-done | bytes 524320 | tf_op jit(solution)/shard_map/all_to_all | solution.py:17
  221.2 0.1 reshape.77
  221.4 0.1 copy.23
  221.5 0.8 reshape.86
  222.3 5.3 %all-to-all-start.2 = ((f32[32,1,512]{2,1,0:T(1,128)}), f32[32,1,512]{2,1,0:T(1,128)S(1)}, u32[]{:S(2)}, u32[]{:S(2)}) async-start(f32[32,1,512]{2,1,0:T(1,128)} %reshape.86), calls=%async_computation.2 | async-start | bytes 131072 | tf_op jit(solution)/shard_map/all_to_all | solution.py:54
  227.5 0.0 copy-done.3
  227.5 0.1 add_divide_fusion
  227.6 8.7 %all-to-all-done.2 = f32[32,1,512]{2,1,0:T(1,128)S(1)} async-done(((f32[32,1,512]{2,1,0:T(1,128)}), f32[32,1,512]{2,1,0:T(1,128)S(1)}, u32[]{:S(2)}, u32[]{:S(2)}) %all-to-all-start.2) | async-done | bytes 65568 | tf_op jit(solution)/shard_map/all_to_all | solution.py:54
  236.4 0.5 broadcast.20
  236.9 0.8 reduce
  237.7 0.1 reshape.87
  237.8 0.1 copy.25
  237.9 0.0 copy-done
  237.9 0.4 convolution_multiply_fusion
  238.3 0.3 fusion.3
  238.7 0.1 copy.35
  238.7 0.1 reshape.88
  238.9 12.0 %all_to_all.34 = f32[32,1,512]{2,1,0:T(1,128)S(1)} all-to-all(f32[32,1,512]{2,1,0:T(1,128)S(1)} %reshape.88), channel_id=1, replica_groups=mesh['row'=8,'col'=32] {'col'}, dimensions={0} | all-to-all | bytes 131072 | tf_op jit(solution)/shard_map/all_to_all | solution.py:64
  250.9 0.8 reduce.1
  251.7 0.1 reshape.89
  251.7 0.1 copy.30
  251.9 0.1 reshape.82
  252.0 0.0 copy-start.2
  252.0 12.3 %all_to_all.35 = bf16[8,64,256]{2,1,0:T(8,128)(2,1)S(1)} all-to-all(bf16[8,64,256]{2,1,0:T(8,128)(2,1)S(1)} %broadcast_in_dim.2), channel_id=1, replica_groups=mesh['row'=8,'col'=32] {'row'}, dimensions={0} | all-to-all | bytes 524288 | tf_op jit(solution)/shard_map/all_to_all | solution.py:29
  264.3 7.7 %fusion = bf16[8192,256]{0,1:T(8,128)(2,1)} fusion(bf16[512,256]{1,0:T(8,128)(2,1)S(1)} %bitcast.47, bf16[8192,512]{0,1:T(8,128)(2,1)} %bitcast.46), kind=kOutput, calls=%fused_computation.1 | convolution fusion | flops 2149580800 | bytes 12845056 | tf_op jit(solution)/shard_map/dot_general | solution.py:68
  272.0 6.4 %copy.31 = bf16[8192,256]{1,0:T(8,128)(2,1)} copy(bf16[8192,256]{0,1:T(8,128)(2,1)} %fusion) | data formatting | bytes 8388608
  278.4 0.0 copy-done.2
  (6 shorter events, 0.1 us)
Async XLA Ops:
  0.6 237.3 %copy-start = (f32[128,128]{1,0:T(8,128)S(1)}, f32[128,128]{1,0:T(8,128)}, u32[]{:S(2)}) copy-start(f32[128,128]{1,0:T(8,128)} %param.9) | copy-start | bytes 196612
  2.6 198.8 %copy-start.4 = (bf16[8192,256]{1,0:T(8,128)(2,1)S(1)}, bf16[8192,256]{1,0:T(8,128)(2,1)}, u32[]{:S(2)}) copy-start(bf16[8192,256]{1,0:T(8,128)(2,1)} %param.6) | copy-start | bytes 12582916
  198.2 3.2 %copy-start.1 = (bf16[32,8192,16]{1,2,0:T(8,128)(2,1)}, bf16[32,8192,16]{1,2,0:T(8,128)(2,1)S(1)}, u32[]{:S(2)}) copy-start(bf16[32,8192,16]{1,2,0:T(8,128)(2,1)S(1)} %all_to_all.33) | copy-start | bytes 25165828
  201.5 26.1 %copy-start.3 = (f32[128]{0:T(128)S(1)}, f32[128]{0:T(128)}, u32[]{:S(2)}) copy-start(f32[128]{0:T(128)} %param.8) | copy-start | bytes 1540
  204.6 16.6 %all-to-all-start.1 = ((f32[8,64,256]{2,1,0:T(8,128)}), f32[8,64,256]{2,1,0:T(8,128)S(1)}, u32[]{:S(2)}, u32[]{:S(2)}) async-start(f32[8,64,256]{2,1,0:T(8,128)} %fusion.1), calls=%async_computation.1 | async-start | bytes 1048576 | tf_op jit(solution)/shard_map/all_to_all | solution.py:17
  222.3 14.1 %all-to-all-start.2 = ((f32[32,1,512]{2,1,0:T(1,128)}), f32[32,1,512]{2,1,0:T(1,128)S(1)}, u32[]{:S(2)}, u32[]{:S(2)}) async-start(f32[32,1,512]{2,1,0:T(1,128)} %reshape.86), calls=%async_computation.2 | async-start | bytes 131072 | tf_op jit(solution)/shard_map/all_to_all | solution.py:54
  252.0 26.4 %copy-start.2 = (f32[64,256]{1,0:T(8,128)}, f32[64,256]{1,0:T(8,128)S(1)}, u32[]{:S(2)}) copy-start(f32[64,256]{1,0:T(8,128)S(1)} %reshape.82) | copy-start | bytes 196612
